TPU v7x, 32 devices: a whole 2x2x4 slice. The times are simulated.
32 devices in a mesh: group: 4 (over y, x), seq: 8 (over z, core).
Axes of the slice: x: 2, y: 2, z: 4, core: 2. Of those that a mesh axis runs over, the one named last changes fastest.
Arguments:
- tokens: bfloat16 [32, 2048, 2048], P('group', 'seq'), may hold values from -6 to 6
- image_keys: bfloat16 [32, 256, 2048], P('group', 'seq'), may hold values from -256 to 256
- image_values: bfloat16 [32, 256, 2048], P('group', 'seq'), may hold values from -18 to 18
- text_len: int32 [32], replicated, may hold values from 1 to 2048
- image_len: int32 [32], replicated, may hold values from 1 to 256
- counts: int32 [6], replicated, may hold values from 1 to 4, as said below
- old_group: int32 [6], replicated, may hold values from 0 to 3, as said below
- new_group: int32 [6], replicated, may hold values from 0 to 3, as said below
- w_query: bfloat16 [2048, 2048], replicated, may hold values from -0.125 to 0.125
- w_out: bfloat16 [2048, 2048], replicated, may hold values from -0.125 to 0.125
Outputs:
- layer_out: bfloat16 [32, 2048, 2048], P('group', 'seq')
Inputs may be any that keep to these rules, and one draw needn't show every extreme that they name: `counts`: every task has at most 4 samples, and some task has exactly 4. `old_group`: each group is the old group of at most two tasks, and no two tasks share both their old group and their new group, so at most 4 samples go from one old group to one new group. `new_group`: each group is the new group of at most two tasks.
All inputs are finite; a program needn't handle non-finite values.
Results may differ from a plain program's by a relative error of at most 0.011.
Values may be sent and summed in bfloat16 or wider, within the bound.
A program may use at most 128 MiB of HBM per device.

v0:
```python
import jax
import jax.numpy as jnp
from jax import lax
from jax.sharding import PartitionSpec as P

HEAD_DIM = 128
HALF = 4


masked_score = -1e30
norm_eps = 1e-05


def layout(counts, old_group, new_group, group_count, slot_count):
    task_order = jnp.arange(counts.shape[0], dtype=jnp.int32)
    earlier = task_order[None, :] < task_order[:, None]
    same_old = old_group[None, :] == old_group[:, None]
    same_new = new_group[None, :] == new_group[:, None]
    old_start = jnp.sum(jnp.where(earlier & same_old, counts[None, :], 0), axis=1)
    new_start = jnp.sum(jnp.where(earlier & same_new, counts[None, :], 0), axis=1)
    target = jnp.arange(group_count * slot_count, dtype=jnp.int32)
    target_group = target // slot_count
    target_slot = target % slot_count
    matches = (
        (new_group[None, :] == target_group[:, None])
        & (target_slot[:, None] >= new_start[None, :])
        & (target_slot[:, None] < (new_start + counts)[None, :])
    )
    filled = jnp.any(matches, axis=1)
    offset = target_slot - jnp.sum(jnp.where(matches, new_start[None, :], 0), axis=1)
    source_group = jnp.sum(jnp.where(matches, old_group[None, :], 0), axis=1)
    source_slot = jnp.sum(jnp.where(matches, old_start[None, :], 0), axis=1) + offset
    return (filled, source_group, source_slot, offset, old_start)


def normalize(samples_rows):
    values = samples_rows.astype(jnp.float32)
    average = jnp.mean(values, axis=-1, keepdims=True)
    centred = values - average
    variance = jnp.mean(centred * centred, axis=-1, keepdims=True)
    return (centred * lax.rsqrt(variance + norm_eps)).astype(jnp.bfloat16)


def spread_rows(source_array, source_index, wanted):
    gathered = jnp.take(source_array, source_index, axis=0)
    return jnp.where(wanted[:, None, None], gathered, jnp.zeros((), source_array.dtype))


def regroup(joined, group_index, group_count, slot_count, tables, counts, old_group, new_group):
    filled, source_group, source_slot, offset, old_start = tables
    own_first = group_index * slot_count
    filled_here = lax.dynamic_slice_in_dim(filled, own_first, slot_count)
    from_group = lax.dynamic_slice_in_dim(source_group, own_first, slot_count)
    destinations = jnp.arange(group_count, dtype=jnp.int32)
    pairing = (old_group[None, :] == group_index) & (new_group[None, :] == destinations[:, None])
    pair_first = jnp.sum(jnp.where(pairing, old_start[None, :], 0), axis=1)
    pair_amount = jnp.sum(jnp.where(pairing, counts[None, :], 0), axis=1)
    position = jnp.arange(HALF, dtype=jnp.int32)
    sending = (position[None, :] < pair_amount[:, None]).reshape(-1)
    source_index = jnp.where(sending, (pair_first[:, None] + position[None, :]).reshape(-1), 0)
    outgoing = spread_rows(joined, source_index, sending)
    incoming = lax.all_to_all(outgoing, "group", split_axis=0, concat_axis=0, tiled=True)
    chosen = from_group * HALF + lax.dynamic_slice_in_dim(offset, own_first, slot_count)
    chosen = jnp.where(filled_here, chosen, 0)
    return spread_rows(incoming, chosen, filled_here)


def cross_layer(
    samples_rows, key_rows, value_rows, text_limit, key_limit, w_query, w_out, first_row
):
    slot_count, row_count, feature_count = samples_rows.shape
    head_count = w_query.shape[1] // HEAD_DIM
    normal = normalize(samples_rows).reshape(slot_count * row_count, feature_count)
    queries = (
        jnp.dot(normal, w_query, preferred_element_type=jnp.float32) * HEAD_DIM ** (-0.5)
    ).astype(jnp.bfloat16)
    queries = queries.reshape(slot_count, row_count, head_count, HEAD_DIM)
    running_max = jnp.full((slot_count, head_count, row_count), masked_score, jnp.float32)
    piece_keys = lax.all_gather(key_rows, "seq", axis=1, tiled=True)
    piece_values = lax.all_gather(value_rows, "seq", axis=1, tiled=True)
    key_count = piece_keys.shape[1]
    head_keys = piece_keys.reshape(slot_count, key_count, head_count, HEAD_DIM)
    head_values = piece_values.reshape(slot_count, key_count, head_count, HEAD_DIM)
    scores = jnp.einsum("sqhd,skhd->shqk", queries, head_keys, preferred_element_type=jnp.float32)
    position = jnp.arange(key_count, dtype=jnp.int32)
    allowed = (position[None, :] < key_limit[:, None])[:, None, None, :]
    scores = jnp.where(allowed, scores, masked_score)
    new_max = jnp.maximum(running_max, jnp.max(scores, axis=-1))
    probs = jnp.where(allowed, jnp.exp(scores - new_max[..., None]), 0.0)
    running_sum = jnp.sum(probs, axis=-1)
    weights = probs.astype(jnp.bfloat16)
    running_ctx = jnp.einsum(
        "shqk,skhd->shqd", weights, head_values, preferred_element_type=jnp.float32
    )
    running_max, running_sum, running_ctx = (new_max, running_sum, running_ctx)
    context = running_ctx / running_sum[..., None]
    context = (
        context.transpose(0, 2, 1, 3)
        .reshape(slot_count * row_count, head_count * HEAD_DIM)
        .astype(jnp.bfloat16)
    )
    projected = jnp.dot(context, w_out, preferred_element_type=jnp.float32).reshape(
        slot_count, row_count, feature_count
    )
    row_position = first_row + jnp.arange(row_count, dtype=jnp.int32)
    kept_rows = row_position[None, :] < text_limit[:, None]
    return jnp.where(kept_rows[..., None], projected, 0.0).astype(jnp.bfloat16)


def on_device(
    tokens,
    image_keys,
    image_values,
    text_len,
    image_len,
    counts,
    old_group,
    new_group,
    w_query,
    w_out,
):
    group_count = lax.axis_size("group")
    slot_count = tokens.shape[0]
    row_count = tokens.shape[1]
    group_index = lax.axis_index("group")
    first_row = lax.axis_index("seq") * row_count
    tables = layout(counts, old_group, new_group, group_count, slot_count)
    own_first = group_index * slot_count
    text_limit = lax.dynamic_slice_in_dim(text_len, own_first, slot_count)
    key_limit = lax.dynamic_slice_in_dim(image_len, own_first, slot_count)
    attended = cross_layer(
        tokens, image_keys, image_values, text_limit, key_limit, w_query, w_out, first_row
    )
    return regroup(
        attended, group_index, group_count, slot_count, tables, counts, old_group, new_group
    )


def solution(mesh):
    in_specs = (
        P("group", "seq", None),
        P("group", "seq", None),
        P("group", "seq", None),
        P(),
        P(),
        P(),
        P(),
        P(),
        P(),
        P(),
    )
    out_specs = P("group", "seq", None)
    return jax.shard_map(
        on_device, mesh=mesh, in_specs=in_specs, out_specs=out_specs, check_vma=False
    )
```

profile of v0, /device:TPU:0, one launch (start us, length us, event | category | flops | bytes accessed | tf_op | source)
XLA Modules:
  0.0 466.6 jit_solution(17421429270864026179)
XLA Ops:
  6.5 2.9 copy.28
  9.5 0.7 all-gather.5.cloned.1.call-update
  10.2 4.7 %convert_reduce_fusion = f32[8,256]{1,0:T(8,128)S(1)} fusion(bf16[8,256,2048]{2,1,0:T(8,128)(2,1)} %param.10), kind=kLoop, calls=%fused_computation.7 | loop fusion | flops 8386560 | bytes 8396800 | tf_op jit(solution)/shard_map/reduce_sum | solution.py:38
  14.9 1.1 copy-done
  16.0 2.4 fusion.4
  18.3 2.5 fusion.5
  21.0 19.4 %fusion.21 = bf16[256,8,16,128]{3,1,2,0:T(8,128)(2,1)} fusion(bf16[2048,2048]{1,0:T(8,128)(2,1)S(1)} %bitcast.27, bf16[2048,2048]{1,0:T(8,128)(2,1)S(1)} %bitcast.31), kind=kOutput, calls=%fused_computation.27 | convolution fusion | flops 17188257792 | bytes 25165824 | tf_op jit(solution)/shard_map/dot_general | solution.py:75
  40.3 9.8 %copy.38 = bf16[256,8,16,128]{3,2,1,0:T(8,128)(2,1)} copy(bf16[256,8,16,128]{3,1,2,0:T(8,128)(2,1)} %fusion.21) | data formatting | bytes 16777216
  50.1 0.1 dynamic_slice.19
  50.2 0.1 dynamic_slice.18
  50.3 0.2 select_reduce_fusion.4
  50.5 0.2 select_reduce_fusion.6
  50.7 0.1 iota_add_fusion
  50.8 0.1 select_n.139
  50.8 0.1 add.104
  51.0 0.1 lt.144
  51.3 43.1 %all-gather.3.cloned.1.call-done = bf16[8,256,2048]{2,0,1:T(8,128)(2,1)} async-done(((bf16[8,32,2048]{2,0,1:T(8,128)(2,1)}), bf16[8,256,2048]{2,0,1:T(8,128)(2,1)}) %all-gather.3.cloned.1.call-update) | async-done | bytes 8388624 | tf_op jit(solution)/shard_map/all_gather | solution.py:79
  94.3 13.0 %copy.29 = bf16[8,256,2048]{1,2,0:T(8,128)(2,1)} copy(bf16[8,256,2048]{2,0,1:T(8,128)(2,1)} %all-gather.3.cloned.1.call-done) | data formatting | bytes 16777216 | tf_op jit(solution)/shard_map/all_gather | solution.py:79
  107.3 21.7 %select_reduce_fusion = (f32[8,16,256]{2,1,0:T(8,128)S(1)}, f32[8,16,256,256]{2,3,1,0:T(8,128)}) fusion(pred[8,256]{1,0:T(8,128)(4,1)S(1)} %iota_compare_fusion, bf16[8,256,16,128]{1,3,2,0:T(8,128)(2,1)} %bitcast.26, bf16[8,256,16,128]{3,2,1,0:T(8,128)(2,1)} %bitcast.25), kind=kOutput, calls=%fused_computation.3 | convolution fusion | flops 2164228096 | bytes 50464768 | tf_op jit(solution)/shard_map/sqhd,skhd->shqk/dot_general | solution.py:84
  129.1 14.7 %fusion = f32[8,16,256]{2,1,0:T(8,128)S(1)} fusion(f32[8,16,256,256]{2,3,1,0:T(8,128)} %get-tuple-element.18, f32[8,16,256]{2,1,0:T(8,128)S(1)} %broadcast_maximum_fusion, pred[8,256]{1,0:T(8,128)(4,1)S(1)} %iota_compare_fusion), kind=kLoop, calls=%fused_computation.4 | loop fusion | flops 33521664 | bytes 33818624 | tf_op jit(solution)/shard_map/reduce_sum | solution.py:90
  143.8 32.7 %all-gather.5.cloned.1.call-done = bf16[8,256,2048]{2,1,0:T(8,128)(2,1)} async-done(((bf16[8,32,2048]{2,1,0:T(8,128)(2,1)}), bf16[8,256,2048]{2,1,0:T(8,128)(2,1)}) %all-gather.5.cloned.1.call-update) | async-done | bytes 8388624 | tf_op jit(solution)/shard_map/all_gather | solution.py:80
  176.5 11.3 %copy.32 = bf16[8,256,2048]{1,2,0:T(8,128)(2,1)} copy(bf16[8,256,2048]{2,1,0:T(8,128)(2,1)} %all-gather.5.cloned.1.call-done) | data formatting | bytes 16777216 | tf_op jit(solution)/shard_map/all_gather | solution.py:80
  187.8 17.3 %fusion.8 = bf16[8,256,16,128]{1,3,2,0:T(8,128)(2,1)S(1)} fusion(f32[8,256,16]{1,2,0:T(8,128)S(1)} %bitcast.29, bf16[8,256,16,128]{1,3,2,0:T(8,128)(2,1)} %bitcast.28, f32[8,16,256,256]{2,3,1,0:T(8,128)} %get-tuple-element.18, f32[8,16,256]{2,1,0:T(8,128)S(1)} %broadcast_maximum_fusion, pred[8,256]{1,0:T(8,128)(4,1)S(1)} %iota_compare_fusion), kind=kOutput, calls=%fused_computation.14 | convolution fusion | flops 2189426688 | bytes 50595840 | tf_op jit(solution)/shard_map/shqk,skhd->shqd/dot_general | solution.py:92
  205.1 21.7 %select_convert_fusion = bf16[8,256,2048]{2,1,0:T(8,128)(2,1)} fusion(pred[8,256]{1,0:T(8,128)(4,1)S(1)} %broadcast_compare_fusion, bf16[8,256,2048]{1,2,0:T(8,128)(2,1)S(1)} %bitcast.32, bf16[2048,2048]{1,0:T(8,128)(2,1)} %param.19), kind=kOutput, calls=%fused_computation.16 | convolution fusion | flops 17188257792 | bytes 25167872 | tf_op jit(solution)/shard_map/dot_general | solution.py:102
  226.8 10.5 %gather_fusion = bf16[16,256,2048]{2,1,0:T(8,128)(2,1)} fusion(bf16[8,256,2048]{2,1,0:T(8,128)(2,1)} %select_convert_fusion, s32[1024]{0:T(1024)S(1)} %pad_clamp_fusion.1), kind=kCustom, calls=%fused_computation | custom fusion | bytes 33554496 | tf_op jit(solution)/shard_map/jit(_take)/gather | solution.py:45
  237.3 14.3 %select_select_fusion = bf16[16,256,2048]{2,1,0:T(8,128)(2,1)} fusion(bf16[16,256,2048]{2,1,0:T(8,128)(2,1)} %gather_fusion, pred[16]{0:T(512)(128)(4,1)S(1)} %compare_and_fusion.1, pred[16]{0:T(512)(128)(4,1)S(1)} %lt.144), kind=kLoop, calls=%fused_computation.15 | loop fusion | flops 16777216 | bytes 33554464 | tf_op jit(solution)/shard_map/jit(_where)/select_n | solution.py:46
  251.6 7.0 %all-to-all-start = ((bf16[16,256,2048]{2,1,0:T(8,128)(2,1)}), bf16[16,256,2048]{2,1,0:T(8,128)(2,1)}, u32[]{:S(2)}, u32[]{:S(2)}) async-start(bf16[16,256,2048]{2,1,0:T(8,128)(2,1)} %select_select_fusion), calls=%async_computation | async-start | bytes 33554432 | tf_op jit(solution)/shard_map/all_to_all | solution.py:62
  258.5 0.1 select_reduce_fusion.3
  258.7 0.1 compare_and_fusion.2
  258.8 182.7 %all-to-all-done = bf16[16,256,2048]{2,1,0:T(8,128)(2,1)} async-done(((bf16[16,256,2048]{2,1,0:T(8,128)(2,1)}), bf16[16,256,2048]{2,1,0:T(8,128)(2,1)}, u32[]{:S(2)}, u32[]{:S(2)}) %all-to-all-start) | async-done | bytes 16777248 | tf_op jit(solution)/shard_map/all_to_all | solution.py:62
  441.4 10.5 %gather_fusion.1 = bf16[8,256,2048]{2,1,0:T(8,128)(2,1)} fusion(bf16[16,256,2048]{2,1,0:T(8,128)(2,1)} %all-to-all-done, s32[1024]{0:T(1024)S(1)} %pad_clamp_fusion), kind=kCustom, calls=%fused_computation.1 | custom fusion | bytes 16777248 | tf_op jit(solution)/shard_map/jit(_take)/gather | solution.py:45
  452.0 7.7 %select_select_fusion.1 = bf16[8,256,2048]{2,1,0:T(8,128)(2,1)} fusion(bf16[8,256,2048]{2,1,0:T(8,128)(2,1)} %gather_fusion.1, pred[8]{0:T(512)(128)(4,1)S(1)} %get-tuple-element.11, pred[8]{0:T(512)(128)(4,1)S(1)} %get-tuple-element.13), kind=kLoop, calls=%fused_computation.26 | loop fusion | flops 8388608 | bytes 16777232 | tf_op jit(solution)/shard_map/jit(_where)/select_n | solution.py:46
  (35 shorter events, 0.5 us)
Async XLA Ops:
  6.5 87.8 %all-gather.3.cloned.1.call-start = ((), (), s32[]{:S(2)}) async-start(), calls=%async_computation.1 | async-start | bytes 9437184 | tf_op jit(solution)/shard_map/all_gather | solution.py:79
  9.4 167.1 %all-gather.5.cloned.1.call-start = ((), (), s32[]{:S(2)}) async-start(), calls=%async_computation.2 | async-start | bytes 9437184 | tf_op jit(solution)/shard_map/all_gather | solution.py:80
  10.2 5.8 %copy-start = (bf16[8,256,2048]{2,1,0:T(8,128)(2,1)S(1)}, bf16[8,256,2048]{2,1,0:T(8,128)(2,1)}, u32[]{:S(2)}) copy-start(bf16[8,256,2048]{2,1,0:T(8,128)(2,1)} %param.10) | copy-start | bytes 25165828
  16.0 4.9 %slice-start = ((s8[8388608]{0:T(1024)(128)(4,1)}), s8[4194304]{0:T(1024)(128)(4,1)S(1)}, s32[]{:S(2)}) async-start(s8[8388608]{0:T(1024)(128)(4,1)} %bitcast.30), calls=%async_computation.3 | async-start | bytes 8388608
  18.3 2.6 slice-start.1
  40.3 9.8 %copy-start.4 = (s32[32]{0:T(128)S(1)}, s32[32]{0:T(128)}, u32[]{:S(2)}) copy-start(s32[32]{0:T(128)} %param.14) | copy-start | bytes 388
  40.3 9.9 %copy-start.5 = (s32[32]{0:T(128)S(1)}, s32[32]{0:T(128)}, u32[]{:S(2)}) copy-start(s32[32]{0:T(128)} %param.13) | copy-start | bytes 388
  40.3 10.0 %copy-start.1 = (s32[6]{0:T(128)S(1)}, s32[6]{0:T(128)}, u32[]{:S(2)}) copy-start(s32[6]{0:T(128)} %param.17) | copy-start | bytes 76
  40.3 10.0 %copy-start.2 = (s32[6]{0:T(128)S(1)}, s32[6]{0:T(128)}, u32[]{:S(2)}) copy-start(s32[6]{0:T(128)} %param.16) | copy-start | bytes 76
  40.3 10.0 %copy-start.3 = (s32[6]{0:T(128)S(1)}, s32[6]{0:T(128)}, u32[]{:S(2)}) copy-start(s32[6]{0:T(128)} %param.15) | copy-start | bytes 76
  251.6 189.9 %all-to-all-start = ((bf16[16,256,2048]{2,1,0:T(8,128)(2,1)}), bf16[16,256,2048]{2,1,0:T(8,128)(2,1)}, u32[]{:S(2)}, u32[]{:S(2)}) async-start(bf16[16,256,2048]{2,1,0:T(8,128)(2,1)} %select_select_fusion), calls=%async_computation | async-start | bytes 33554432 | tf_op jit(solution)/shard_map/all_to_all | solution.py:62
Sparse Core Ops, SparseCore 0:
  9.6 84.7 all-gather.2
  95.9 80.5 all-gather.4
where the time goes:
time: 468 us; the launch traced here: 467 us
  waiting for transfers between devices  259 us (55%)
  matrix products  80.1 us (17%)
  local copies, waits for them, and re-layouts  59.5 us (13%)
  other arithmetic  47.2 us (10%)
  between operations  13.6 us (3%)
  starting transfers between devices  7 us (1%)
    all_to_all x1, waiting for transfers between devices, regroup(): lax.all_to_all(outgoing, 'group', split_axis=0, concat_axis=0, tiled=True)  183 us
    all_gather x1, waiting for transfers between devices, cross_layer(): piece_keys = lax.all_gather(key_rows, 'seq', axis=1, tiled=True)  43.1 us
    all_gather x1, waiting for transfers between devices, cross_layer(): piece_values = lax.all_gather(value_rows, 'seq', axis=1, tiled=True)  32.7 us
    select_n x2, other arithmetic, spread_rows(): jnp.where(wanted[:, None, None], gathered, jnp.zeros((), source_array.dty...  22 us
    dot_general x1, matrix products, cross_layer(): jnp.einsum('sqhd,skhd->shqk', queries, head_keys, preferred_element_type=...  21.7 us
    dot_general x1, matrix products, cross_layer(): jnp.dot(context, w_out, preferred_element_type=jnp.float32)  21.7 us
    gather x2, local copies, waits for them, and re-layouts, spread_rows(): gathered = jnp.take(source_array, source_index, axis=0)  21 us
    dot_general x1, matrix products, cross_layer(): jnp.dot(normal, w_query, preferred_element_type=jnp.float32)  19.4 us
  transfers between devices with their start and end apart: 3, of which 3 were waited for; matrix products, arithmetic and copies ran while one was open for 19% of the time, Pallas kernels for 0%

commit v1 on v0

v1 whole, which is shorter than its diff:
```python
import functools

import jax
import jax.numpy as jnp
from jax import lax
from jax.experimental import pallas as pl
from jax.experimental.pallas import tpu as pltpu
from jax.sharding import PartitionSpec as P

HEAD_DIM = 128
PAIR = 2
HEADS_AT_ONCE = 4
OUT_TILE = 512

masked_score = -1e30
norm_eps = 1e-05


def pick_tasks(own, other, counts, group_index):
    order = jnp.arange(counts.shape[0], dtype=jnp.int32)
    earlier = (order[None, :] < order[:, None]) & (own[None, :] == own[:, None])
    start = jnp.sum(jnp.where(earlier, counts[None, :], 0), axis=1)
    rank = jnp.sum(earlier.astype(jnp.int32), axis=1)
    lanes = jnp.arange(PAIR, dtype=jnp.int32)
    mine = (own == group_index)[None, :] & (rank[None, :] == lanes[:, None])

    def chosen(values):
        return jnp.sum(jnp.where(mine, values[None, :], 0), axis=1)

    return chosen(counts), chosen(start), chosen(other)


def old_tables(counts, old_group, new_group, group_index, group_count, half):
    size, start, target = pick_tasks(old_group, new_group, counts, group_index)
    step = jnp.arange(half, dtype=jnp.int32)[:, None]
    valid = step < size[None, :]
    slot = jnp.where(valid, start[None, :] + step, 0)
    first = jnp.where(valid[:, 0], target[0], (target[1] + 1) % group_count)
    second = jnp.where(valid[:, 1], target[1], (first + 1) % group_count)
    return valid, slot, jnp.stack([first, second], axis=1)


def new_tables(counts, old_group, new_group, group_index, half):
    size, start, source = pick_tasks(new_group, old_group, counts, group_index)
    step = jnp.arange(half, dtype=jnp.int32)[:, None]
    valid = step < size[None, :]
    empty = (~valid).reshape(-1).astype(jnp.int32)
    spare = (jnp.cumsum(empty) - empty).reshape(half, PAIR) + jnp.sum(size)
    slot = jnp.where(valid, start[None, :] + step, spare)
    return valid, slot, jnp.broadcast_to(source[None, :], valid.shape)


def normalize(samples_rows):
    values = samples_rows.astype(jnp.float32)
    average = jnp.mean(values, axis=-1, keepdims=True)
    centred = values - average
    variance = jnp.mean(centred * centred, axis=-1, keepdims=True)
    return (centred * lax.rsqrt(variance + norm_eps)).astype(jnp.bfloat16)


def attend_kernel(table, q_ref, k_ref, v_ref, w_hbm, out_ref, w_ref, ctx_ref, sem):
    lane = pl.program_id(0)
    rows, width = ctx_ref.shape
    seq_count, piece = k_ref.shape[0], k_ref.shape[1]
    keys = seq_count * piece
    load = pltpu.make_async_copy(w_hbm, w_ref, sem)

    @pl.when(lane == 0)
    def _():
        load.start()

    valid = table[0, lane] > 0
    key_limit = table[3, lane]
    row_limit = table[4, lane]

    @pl.when(valid)
    def _():
        allowed = lax.broadcasted_iota(jnp.int32, (rows, keys), 1) < key_limit

        def some_heads(block, carry):
            for inner in range(HEADS_AT_ONCE):
                first = pl.multiple_of((block * HEADS_AT_ONCE + inner) * HEAD_DIM, HEAD_DIM)
                columns = pl.ds(first, HEAD_DIM)
                key = k_ref[:, :, columns].reshape(keys, HEAD_DIM)
                value = v_ref[:, :, columns].reshape(keys, HEAD_DIM)
                scores = lax.dot_general(
                    q_ref[0, :, columns],
                    key,
                    (((1,), (1,)), ((), ())),
                    preferred_element_type=jnp.float32,
                )
                scores = jnp.where(allowed, scores, masked_score)
                top = jnp.max(scores, axis=-1, keepdims=True)
                probs = jnp.where(allowed, jnp.exp(scores - top), 0.0)
                total = jnp.sum(probs, axis=-1, keepdims=True)
                context = jnp.dot(
                    probs.astype(jnp.bfloat16), value, preferred_element_type=jnp.float32
                )
                ctx_ref[:, columns] = (context / total).astype(jnp.bfloat16)
            return carry

        lax.fori_loop(0, width // (HEAD_DIM * HEADS_AT_ONCE), some_heads, 0)

    @pl.when(lane == 0)
    def _():
        load.wait()

    @pl.when(valid)
    def _():
        features = out_ref.shape[2]
        kept = lax.broadcasted_iota(jnp.int32, (rows, OUT_TILE), 0) < row_limit

        def some_columns(block, carry):
            columns = pl.ds(pl.multiple_of(block * OUT_TILE, OUT_TILE), OUT_TILE)
            projected = jnp.dot(
                ctx_ref[...], w_ref[:, columns], preferred_element_type=jnp.float32
            )
            out_ref[0, :, columns] = jnp.where(kept, projected, 0.0).astype(jnp.bfloat16)
            return carry

        lax.fori_loop(0, features // OUT_TILE, some_columns, 0)

    @pl.when(jnp.logical_not(valid))
    def _():
        out_ref[...] = jnp.zeros_like(out_ref)


def attend(table, queries, gathered, w_out, group_count):
    _, rows, width = queries.shape
    seq_count, packed, _ = gathered.shape
    piece = packed // (2 * PAIR)
    features = w_out.shape[1]
    keys = seq_count * piece
    return pl.pallas_call(
        attend_kernel,
        name="attend",
        out_shape=jax.ShapeDtypeStruct((group_count, rows, features), jnp.bfloat16),
        grid_spec=pltpu.PrefetchScalarGridSpec(
            num_scalar_prefetch=1,
            grid=(PAIR,),
            in_specs=[
                pl.BlockSpec((1, rows, width), lambda a, t: (t[1, a], 0, 0)),
                pl.BlockSpec((seq_count, piece, width), lambda a, t: (0, a, 0)),
                pl.BlockSpec((seq_count, piece, width), lambda a, t: (0, PAIR + a, 0)),
                pl.BlockSpec(memory_space=pl.ANY),
            ],
            out_specs=pl.BlockSpec((1, rows, features), lambda a, t: (t[2, a], 0, 0)),
            scratch_shapes=[
                pltpu.VMEM(w_out.shape, jnp.bfloat16),
                pltpu.VMEM((rows, width), jnp.bfloat16),
                pltpu.SemaphoreType.DMA,
            ],
        ),
        compiler_params=pltpu.CompilerParams(
            dimension_semantics=("arbitrary",), vmem_limit_bytes=40 * 1024 * 1024
        ),
        cost_estimate=pl.CostEstimate(
            flops=PAIR * 2 * rows * width * (2 * keys + features),
            bytes_accessed=2 * (w_out.size + PAIR * (2 * rows + 2 * keys) * width),
            transcendentals=PAIR * rows * keys * (width // HEAD_DIM),
        ),
    )(table, queries, gathered, gathered, w_out)


def place_kernel(table, in_ref, *rest):
    out_ref = rest[-1]
    lane = pl.program_id(0)
    valid = table[0, lane] > 0

    @pl.when(valid)
    def _():
        out_ref[...] = in_ref[...]

    @pl.when(jnp.logical_not(valid))
    def _():
        out_ref[...] = jnp.zeros_like(out_ref)


def place(table, incoming, result, slot_count):
    _, rows, features = incoming.shape
    block = (1, rows, features)
    earlier = () if result is None else (result,)
    return pl.pallas_call(
        place_kernel,
        name="place",
        out_shape=jax.ShapeDtypeStruct((slot_count, rows, features), jnp.bfloat16),
        grid_spec=pltpu.PrefetchScalarGridSpec(
            num_scalar_prefetch=1,
            grid=(PAIR,),
            in_specs=[pl.BlockSpec(block, lambda a, t: (t[2, a], 0, 0))]
            + [pl.BlockSpec(memory_space=pl.ANY)] * len(earlier),
            out_specs=pl.BlockSpec(block, lambda a, t: (t[1, a], 0, 0)),
        ),
        input_output_aliases={2: 0} if earlier else {},
        compiler_params=pltpu.CompilerParams(dimension_semantics=("arbitrary",)),
        cost_estimate=pl.CostEstimate(
            flops=0, bytes_accessed=4 * PAIR * rows * features, transcendentals=0
        ),
    )(table, incoming, *earlier)


def on_device(
    tokens,
    image_keys,
    image_values,
    text_len,
    image_len,
    counts,
    old_group,
    new_group,
    w_query,
    w_out,
):
    group_count = lax.axis_size("group")
    slot_count, row_count, features = tokens.shape
    half = slot_count // PAIR
    piece = image_keys.shape[1]
    width = w_query.shape[1]
    group_index = lax.axis_index("group")
    first_row = lax.axis_index("seq") * row_count
    own_first = group_index * slot_count
    text_limit = lax.dynamic_slice_in_dim(text_len, own_first, slot_count) - first_row
    key_limit = lax.dynamic_slice_in_dim(image_len, own_first, slot_count)

    old_valid, old_slot, old_target = old_tables(
        counts, old_group, new_group, group_index, group_count, half
    )
    new_valid, new_slot, new_source = new_tables(counts, old_group, new_group, group_index, half)
    old_table = jnp.stack(
        [
            old_valid.astype(jnp.int32),
            old_slot,
            old_target,
            jnp.take(key_limit, old_slot),
            jnp.take(text_limit, old_slot),
        ],
        axis=1,
    )
    new_table = jnp.stack([new_valid.astype(jnp.int32), new_slot, new_source], axis=1)

    gathered = []
    for step in range(half):
        pieces = [
            lax.dynamic_index_in_dim(rows, old_slot[step, lane], 0, keepdims=False)
            for rows in (image_keys, image_values)
            for lane in range(PAIR)
        ]
        packed = jnp.concatenate(pieces, axis=0)
        gathered.append(lax.all_gather(packed, "seq", axis=0, tiled=False))

    normal = normalize(tokens).reshape(slot_count * row_count, features)
    queries = (
        jnp.dot(normal, w_query, preferred_element_type=jnp.float32) * HEAD_DIM ** (-0.5)
    ).astype(jnp.bfloat16)
    queries = queries.reshape(slot_count, row_count, width)

    result = None
    for step in range(half):
        outgoing = attend(old_table[step], queries, gathered[step], w_out, group_count)
        incoming = lax.all_to_all(outgoing, "group", split_axis=0, concat_axis=0, tiled=True)
        result = place(new_table[step], incoming, result, slot_count)
    return result


def solution(mesh):
    rows = P("group", "seq", None)
    return jax.shard_map(
        on_device,
        mesh=mesh,
        in_specs=(rows, rows, rows) + (P(),) * 7,
        out_specs=rows,
        check_vma=False,
    )
```

time: 468 us -> 323 us (0.69)
  waiting for transfers between devices: 259 us -> 147 us
  matrix products: 80.1 us -> 19.5 us
  Pallas kernels: 0 us -> 47.2 us
  local copies, waits for them, and re-layouts: 59.5 us -> 27.5 us
  other arithmetic: 47.2 us -> 27.3 us
  starting transfers between devices: 7 us -> 24.4 us
  between operations: 13.6 us -> 28.8 us
    all_to_all x1 -> x4, waiting for transfers between devices: 183 us -> 80.8 us  [on_device(): lax.all_to_all(outgoing, 'group', split_axis=0, concat_axis=0, tiled=True)]
    dot_general x4 -> x1, matrix products: 80.1 us -> 19.5 us  [on_device(): jnp.dot(normal, w_query, preferred_element_type=jnp.float32)]
    pallas_call x0 -> x8, Pallas kernels: none -> 47.2 us  [the longest x4 33.8 us: attend(): pl.pallas_call(attend_kernel, name='attend', out_shape=jax.ShapeDtypeStru...]
    all_gather x2 -> x0, local copies, waits for them, and re-layouts: 24.3 us -> none  [the longest x1 13 us: cross_layer(): piece_keys = lax.all_gather(key_rows, 'seq', axis=1, tiled=True)]
    select_n x4, other arithmetic: 22 us -> 1.98 us  [the longest x1 1.28 us: old_tables(): first = jnp.where(valid[:, 0], target[0], (target[1] + 1) % group_count)]
    gather x2 -> x4, local copies, waits for them, and re-layouts: 21 us -> 1.46 us  [the longest x2 0.73 us: on_device(): jnp.take(key_limit, old_slot)]
    all_to_all x1 -> x4, starting transfers between devices: 6.96 us -> 24.3 us  [on_device(): lax.all_to_all(outgoing, 'group', split_axis=0, concat_axis=0, tiled=True)]
    reduce_sum x4 -> x2, other arithmetic: 15.2 us -> 2.42 us  [the longest x1 1.47 us: chosen(): return jnp.sum(jnp.where(mine, values[None, :], 0), axis=1)]
  transfers between devices with their start and end apart: 3 -> 8, of which waited for: 3 -> 8; matrix products, arithmetic and copies ran while one was open for 19% -> 14% of each run, Pallas kernels for 0% -> 14%
where the time goes in v1:
time: 323 us; the launch traced here: 321 us
  waiting for transfers between devices  147 us (46%)
  Pallas kernels  47.2 us (15%)
  between operations  28.8 us (9%)
  local copies, waits for them, and re-layouts  27.5 us (9%)
  other arithmetic  27.3 us (8%)
  starting transfers between devices  24.4 us (8%)
  matrix products  19.5 us (6%)
    all_to_all x4, waiting for transfers between devices, on_device(): lax.all_to_all(outgoing, 'group', split_axis=0, concat_axis=0, tiled=True)  80.8 us
    all_gather x4, waiting for transfers between devices, on_device(): gathered.append(lax.all_gather(packed, 'seq', axis=0, tiled=False))  65.8 us
    pallas_call x4, Pallas kernels, attend(): pl.pallas_call(attend_kernel, name='attend', out_shape=jax.ShapeDtypeStru...  33.8 us
    all_to_all x4, starting transfers between devices, on_device(): lax.all_to_all(outgoing, 'group', split_axis=0, concat_axis=0, tiled=True)  24.3 us
    dot_general x1, matrix products, on_device(): jnp.dot(normal, w_query, preferred_element_type=jnp.float32)  19.5 us
    unnamed x26, local copies, waits for them, and re-layouts  16.6 us
    pallas_call x4, Pallas kernels, place(): pl.pallas_call(place_kernel, name='place', out_shape=jax.ShapeDtypeStruct...  13.4 us
  transfers between devices with their start and end apart: 8, of which 8 were waited for; matrix products, arithmetic and copies ran while one was open for 14% of the time, Pallas kernels for 14%

profile of v1, /device:TPU:0, one launch (start us, length us, event | category | flops | bytes accessed | tf_op | source)
XLA Modules:
  0.0 321.4 jit_solution(14085982318899363350)
XLA Ops:
  37.2 4.6 %convert_reduce_fusion = f32[8,256]{1,0:T(8,128)S(1)} fusion(bf16[8,256,2048]{2,1,0:T(8,128)(2,1)} %param.12), kind=kLoop, calls=%fused_computation.3 | loop fusion | flops 8386560 | bytes 8396800 | tf_op jit(solution)/shard_map/reduce_sum | solution.py:55
  42.0 6.3 %fusion.2 = f32[8,256]{1,0:T(8,128)S(1)} fusion(bf16[8,256,2048]{2,1,0:T(8,128)(2,1)} %param.12, f32[8,256]{1,0:T(8,128)S(1)} %broadcast_multiply_fusion), kind=kLoop, calls=%fused_computation.6 | loop fusion | flops 16775168 | bytes 8404992 | tf_op jit(solution)/shard_map/reduce_sum | solution.py:57
  48.3 5.5 %fusion.3 = bf16[8,256,2048]{2,1,0:T(8,128)(2,1)S(1)} fusion(bf16[8,256,2048]{2,1,0:T(8,128)(2,1)} %param.12, f32[8,256]{1,0:T(8,128)S(1)} %add_rsqrt_fusion, f32[8,256]{1,0:T(8,128)S(1)} %broadcast_multiply_fusion), kind=kLoop, calls=%fused_computation.7 | loop fusion | flops 16777216 | bytes 16793600 | tf_op jit(solution)/shard_map/convert_element_type | solution.py:58
  53.8 19.5 %multiply_convert_fusion = bf16[2048,2048]{1,0:T(8,128)(2,1)} fusion(bf16[2048,2048]{1,0:T(8,128)(2,1)S(1)} %bitcast.77, bf16[2048,2048]{1,0:T(8,128)(2,1)S(1)} %bitcast.87), kind=kOutput, calls=%fused_computation.8 | convolution fusion | flops 17188257792 | bytes 25165824 | tf_op jit(solution)/shard_map/dot_general | solution.py:253
  73.3 10.9 %all-gather.11.cloned.1.call-done = bf16[1024,2048]{1,0:T(8,128)(2,1)} async-done(((bf16[128,2048]{1,0:T(8,128)(2,1)}), bf16[1024,2048]{1,0:T(8,128)(2,1)}) %all-gather.11.cloned.1.call-update) | async-done | bytes 4194320 | tf_op jit(solution)/shard_map/all_gather | solution.py:249
  84.1 2.2 copy-done.8
  86.3 8.5 %attend.5 = bf16[4,256,2048]{2,1,0:T(8,128)(2,1)S(1)} custom-call(s32[5,2]{1,0:T(8,128)S(1)} %copy.60.table, bf16[8,256,2048]{2,1,0:T(8,128)(2,1)} %bitcast.73, bf16[8,128,2048]{2,1,0:T(8,128)(2,1)S(1)} %bitcast.69, bf16[8,128,2048]{2,1,0:T(8,128)(2,1)S(1)} %bitcast.70, bf16[2048,2048]{1,0:T(8,128)(2,1)} %w_hbm.7), custom_call_target="tpu_custom_call" | custom-call | flops 5368709120 | bytes 16777216 | tf_op jit(solution)/shard_map/attend/pallas_call | solution.py:134
  94.8 1.9 copy-done.3
  96.8 9.7 %all-to-all-start.1 = ((bf16[4,256,2048]{2,1,0:T(8,128)(2,1)}), bf16[4,256,2048]{2,1,0:T(8,128)(2,1)}, u32[]{:S(2)}, u32[]{:S(2)}) async-start(bf16[4,256,2048]{2,1,0:T(8,128)(2,1)} %copy-done.3), calls=%async_computation.1 | async-start | bytes 8388608 | tf_op jit(solution)/shard_map/all_to_all | solution.py:260
  107.6 23.8 %all-gather.13.cloned.1.call-done = bf16[1024,2048]{1,0:T(8,128)(2,1)} async-done(((bf16[128,2048]{1,0:T(8,128)(2,1)}), bf16[1024,2048]{1,0:T(8,128)(2,1)}) %all-gather.13.cloned.1.call-update) | async-done | bytes 4194320 | tf_op jit(solution)/shard_map/all_gather | solution.py:249
  131.4 2.2 copy-done.7
  133.6 8.5 %attend.6 = bf16[4,256,2048]{2,1,0:T(8,128)(2,1)S(1)} custom-call(s32[5,2]{1,0:T(8,128)S(1)} %copy.63.table, bf16[8,256,2048]{2,1,0:T(8,128)(2,1)} %bitcast.74, bf16[8,128,2048]{2,1,0:T(8,128)(2,1)S(1)} %bitcast.67, bf16[8,128,2048]{2,1,0:T(8,128)(2,1)S(1)} %bitcast.68, bf16[2048,2048]{1,0:T(8,128)(2,1)} %w_hbm.7), custom_call_target="tpu_custom_call" | custom-call | flops 5368709120 | bytes 16777216 | tf_op jit(solution)/shard_map/attend/pallas_call | solution.py:134
  142.1 2.0 copy-done.5
  144.1 11.5 %all-to-all-done.1.in_ref = bf16[4,256,2048]{2,1,0:T(8,128)(2,1)} async-done(((bf16[4,256,2048]{2,1,0:T(8,128)(2,1)}), bf16[4,256,2048]{2,1,0:T(8,128)(2,1)}, u32[]{:S(2)}, u32[]{:S(2)}) %all-to-all-start.1) | async-done | bytes 4194336 | tf_op jit(solution)/shard_map/all_to_all | solution.py:260
  155.6 4.8 %all-to-all-start.2 = ((bf16[4,256,2048]{2,1,0:T(8,128)(2,1)}), bf16[4,256,2048]{2,1,0:T(8,128)(2,1)}, u32[]{:S(2)}, u32[]{:S(2)}) async-start(bf16[4,256,2048]{2,1,0:T(8,128)(2,1)} %copy-done.5), calls=%async_computation.2 | async-start | bytes 8388608 | tf_op jit(solution)/shard_map/all_to_all | solution.py:260
  160.6 18.2 %all-gather.15.cloned.1.call-done = bf16[1024,2048]{1,0:T(8,128)(2,1)} async-done(((bf16[128,2048]{1,0:T(8,128)(2,1)}), bf16[1024,2048]{1,0:T(8,128)(2,1)}) %all-gather.15.cloned.1.call-update) | async-done | bytes 4194320 | tf_op jit(solution)/shard_map/all_gather | solution.py:249
  178.8 2.2 copy-done.6
  180.9 8.4 %attend.7 = bf16[4,256,2048]{2,1,0:T(8,128)(2,1)S(1)} custom-call(s32[5,2]{1,0:T(8,128)S(1)} %copy.66.table, bf16[8,256,2048]{2,1,0:T(8,128)(2,1)} %bitcast.75, bf16[8,128,2048]{2,1,0:T(8,128)(2,1)S(1)} %bitcast.65, bf16[8,128,2048]{2,1,0:T(8,128)(2,1)S(1)} %bitcast.66, bf16[2048,2048]{1,0:T(8,128)(2,1)} %w_hbm.7), custom_call_target="tpu_custom_call" | custom-call | flops 5368709120 | bytes 16777216 | tf_op jit(solution)/shard_map/attend/pallas_call | solution.py:134
  189.4 2.0 copy-done.4
  191.4 16.6 %all-to-all-done.2.in_ref = bf16[4,256,2048]{2,1,0:T(8,128)(2,1)} async-done(((bf16[4,256,2048]{2,1,0:T(8,128)(2,1)}), bf16[4,256,2048]{2,1,0:T(8,128)(2,1)}, u32[]{:S(2)}, u32[]{:S(2)}) %all-to-all-start.2) | async-done | bytes 4194336 | tf_op jit(solution)/shard_map/all_to_all | solution.py:260
  207.9 4.9 %all-to-all-start.3 = ((bf16[4,256,2048]{2,1,0:T(8,128)(2,1)}), bf16[4,256,2048]{2,1,0:T(8,128)(2,1)}, u32[]{:S(2)}, u32[]{:S(2)}) async-start(bf16[4,256,2048]{2,1,0:T(8,128)(2,1)} %copy-done.4), calls=%async_computation.3 | async-start | bytes 8388608 | tf_op jit(solution)/shard_map/all_to_all | solution.py:260
  213.0 12.9 %all-gather.9.cloned.1.call-done = bf16[1024,2048]{1,0:T(8,128)(2,1)} async-done(((bf16[128,2048]{1,0:T(8,128)(2,1)}), bf16[1024,2048]{1,0:T(8,128)(2,1)}) %all-gather.9.cloned.1.call-update) | async-done | bytes 4194320 | tf_op jit(solution)/shard_map/all_gather | solution.py:249
  225.9 2.2 copy-done.9
  228.1 8.4 %attend.4 = bf16[4,256,2048]{2,1,0:T(8,128)(2,1)S(1)} custom-call(s32[5,2]{1,0:T(8,128)S(1)} %copy.57.table, bf16[8,256,2048]{2,1,0:T(8,128)(2,1)} %bitcast.76, bf16[8,128,2048]{2,1,0:T(8,128)(2,1)S(1)} %bitcast.71, bf16[8,128,2048]{2,1,0:T(8,128)(2,1)S(1)} %bitcast.72, bf16[2048,2048]{1,0:T(8,128)(2,1)} %w_hbm.7), custom_call_target="tpu_custom_call" | custom-call | flops 5368709120 | bytes 16777216 | tf_op jit(solution)/shard_map/attend/pallas_call | solution.py:134
  236.5 2.0 copy-done.2
  238.5 21.2 %all-to-all-done.3.in_ref = bf16[4,256,2048]{2,1,0:T(8,128)(2,1)} async-done(((bf16[4,256,2048]{2,1,0:T(8,128)(2,1)}), bf16[4,256,2048]{2,1,0:T(8,128)(2,1)}, u32[]{:S(2)}, u32[]{:S(2)}) %all-to-all-start.3) | async-done | bytes 4194336 | tf_op jit(solution)/shard_map/all_to_all | solution.py:260
  259.7 4.9 %all-to-all-start = ((bf16[4,256,2048]{2,1,0:T(8,128)(2,1)}), bf16[4,256,2048]{2,1,0:T(8,128)(2,1)}, u32[]{:S(2)}, u32[]{:S(2)}) async-start(bf16[4,256,2048]{2,1,0:T(8,128)(2,1)} %copy-done.2), calls=%async_computation | async-start | bytes 8388608 | tf_op jit(solution)/shard_map/all_to_all | solution.py:260
  269.9 3.3 %place.4.rest_0_ = bf16[8,256,2048]{2,1,0:T(8,128)(2,1)} custom-call(s32[3,2]{1,0:T(4,128)} %copy.67.table, bf16[4,256,2048]{2,1,0:T(8,128)(2,1)} %all-to-all-done.3.in_ref), custom_call_target="tpu_custom_call" | custom-call | bytes 4194304 | tf_op jit(solution)/shard_map/place/pallas_call | solution.py:183
  273.2 3.3 %place.5.rest_0_ = bf16[8,256,2048]{2,1,0:T(8,128)(2,1)} custom-call(s32[3,2]{1,0:T(4,128)} %copy.68.table, bf16[4,256,2048]{2,1,0:T(8,128)(2,1)} %all-to-all-done.2.in_ref, bf16[8,256,2048]{2,1,0:T(8,128)(2,1)} %place.4.rest_0_), custom_call_target="tpu_custom_call", output_to_operand_aliasing={{}: (2, {})} | custom-call | bytes 4194304 | tf_op jit(solution)/shard_map/place/pallas_call | solution.py:183
  276.6 3.5 %place.6.rest_0_ = bf16[8,256,2048]{2,1,0:T(8,128)(2,1)} custom-call(s32[3,2]{1,0:T(4,128)} %copy.69.table, bf16[4,256,2048]{2,1,0:T(8,128)(2,1)} %all-to-all-done.1.in_ref, bf16[8,256,2048]{2,1,0:T(8,128)(2,1)} %place.5.rest_0_), custom_call_target="tpu_custom_call", output_to_operand_aliasing={{}: (2, {})} | custom-call | bytes 4194304 | tf_op jit(solution)/shard_map/place/pallas_call | solution.py:183
  280.0 31.5 %all-to-all-done.in_ref = bf16[4,256,2048]{2,1,0:T(8,128)(2,1)} async-done(((bf16[4,256,2048]{2,1,0:T(8,128)(2,1)}), bf16[4,256,2048]{2,1,0:T(8,128)(2,1)}, u32[]{:S(2)}, u32[]{:S(2)}) %all-to-all-start) | async-done | bytes 4194336 | tf_op jit(solution)/shard_map/all_to_all | solution.py:260
  311.5 3.3 %place.7 = bf16[8,256,2048]{2,1,0:T(8,128)(2,1)} custom-call(s32[3,2]{1,0:T(4,128)} %copy.70.table, bf16[4,256,2048]{2,1,0:T(8,128)(2,1)} %all-to-all-done.in_ref, bf16[8,256,2048]{2,1,0:T(8,128)(2,1)} %place.6.rest_0_), custom_call_target="tpu_custom_call", output_to_operand_aliasing={{}: (2, {})} | custom-call | bytes 4194304 | tf_op jit(solution)/shard_map/place/pallas_call | solution.py:183
  (87 shorter events, 22.2 us)
Async XLA Ops:
  6.5 7.8 %copy-start = (s32[32]{0:T(128)S(1)}, s32[32]{0:T(128)}, u32[]{:S(2)}) copy-start(s32[32]{0:T(128)} %param.16) | copy-start | bytes 388
  6.5 77.6 %all-gather.11.cloned.1.call-start = ((), (), s32[]{:S(2)}) async-start(), calls=%async_computation.5 | async-start | bytes 4718592 | tf_op jit(solution)/shard_map/all_gather | solution.py:249
  34.8 96.7 %all-gather.13.cloned.1.call-start = ((), (), s32[]{:S(2)}) async-start(), calls=%async_computation.6 | async-start | bytes 4718592 | tf_op jit(solution)/shard_map/all_gather | solution.py:249
  35.8 143.0 %all-gather.15.cloned.1.call-start = ((), (), s32[]{:S(2)}) async-start(), calls=%async_computation.7 | async-start | bytes 4718592 | tf_op jit(solution)/shard_map/all_gather | solution.py:249
  42.0 11.8 %slice-start = ((s8[8388608]{0:T(1024)(128)(4,1)}), s8[4194304]{0:T(1024)(128)(4,1)S(1)}, s32[]{:S(2)}) async-start(s8[8388608]{0:T(1024)(128)(4,1)} %bitcast.86), calls=%async_computation.8 | async-start | bytes 8388608
  48.3 5.5 %slice-start.1 = ((s8[8388608]{0:T(1024)(128)(4,1)}), s8[4194304]{0:T(1024)(128)(4,1)S(1)}, s32[]{:S(2)}) async-start(s8[8388608]{0:T(1024)(128)(4,1)} %bitcast.86), calls=%async_computation.9 | async-start | bytes 8388608
  84.1 2.2 copy-start.8
  94.8 1.9 copy-start.3
  96.8 58.8 %all-to-all-start.1 = ((bf16[4,256,2048]{2,1,0:T(8,128)(2,1)}), bf16[4,256,2048]{2,1,0:T(8,128)(2,1)}, u32[]{:S(2)}, u32[]{:S(2)}) async-start(bf16[4,256,2048]{2,1,0:T(8,128)(2,1)} %copy-done.3), calls=%async_computation.1 | async-start | bytes 8388608 | tf_op jit(solution)/shard_map/all_to_all | solution.py:260
  106.5 119.4 %all-gather.9.cloned.1.call-start = ((), (), s32[]{:S(2)}) async-start(), calls=%async_computation.4 | async-start | bytes 4718592 | tf_op jit(solution)/shard_map/all_gather | solution.py:249
  131.4 2.2 copy-start.7
  142.1 2.0 copy-start.5
  155.6 52.4 %all-to-all-start.2 = ((bf16[4,256,2048]{2,1,0:T(8,128)(2,1)}), bf16[4,256,2048]{2,1,0:T(8,128)(2,1)}, u32[]{:S(2)}, u32[]{:S(2)}) async-start(bf16[4,256,2048]{2,1,0:T(8,128)(2,1)} %copy-done.5), calls=%async_computation.2 | async-start | bytes 8388608 | tf_op jit(solution)/shard_map/all_to_all | solution.py:260
  178.8 2.2 copy-start.6
  189.4 2.0 copy-start.4
  207.9 51.8 %all-to-all-start.3 = ((bf16[4,256,2048]{2,1,0:T(8,128)(2,1)}), bf16[4,256,2048]{2,1,0:T(8,128)(2,1)}, u32[]{:S(2)}, u32[]{:S(2)}) async-start(bf16[4,256,2048]{2,1,0:T(8,128)(2,1)} %copy-done.4), calls=%async_computation.3 | async-start | bytes 8388608 | tf_op jit(solution)/shard_map/all_to_all | solution.py:260
  225.9 2.2 copy-start.9
  236.5 2.0 copy-start.2
  259.7 51.8 %all-to-all-start = ((bf16[4,256,2048]{2,1,0:T(8,128)(2,1)}), bf16[4,256,2048]{2,1,0:T(8,128)(2,1)}, u32[]{:S(2)}, u32[]{:S(2)}) async-start(bf16[4,256,2048]{2,1,0:T(8,128)(2,1)} %copy-done.2), calls=%async_computation | async-start | bytes 8388608 | tf_op jit(solution)/shard_map/all_to_all | solution.py:260
  276.6 38.3 %copy-start.1 = (s32[32]{0:T(128)S(1)}, s32[32]{0:T(128)}, u32[]{:S(2)}) copy-start(s32[32]{0:T(128)} %param.16) | copy-start | bytes 388
Sparse Core Ops, SparseCore 0:
  34.9 49.1 all-gather.10
  85.7 45.6 all-gather.12
  133.0 45.6 all-gather.14
  180.2 45.6 all-gather.8

commit v2 on v1

v2 whole, which is shorter than its diff:
```python
import functools

import jax
import jax.numpy as jnp
from jax import lax
from jax.experimental import pallas as pl
from jax.experimental.pallas import tpu as pltpu
from jax.sharding import PartitionSpec as P

HEAD_DIM = 128
PAIR = 2
HEADS_AT_ONCE = 4
OUT_TILE = 512

masked_score = -1e30
norm_eps = 1e-05


OLD_VALID, OLD_SLOT, OLD_TARGET, OLD_KEYS, OLD_ROWS = range(5)
NEW_VALID, NEW_SLOT, NEW_SOURCE, NEW_KEYS, NEW_ROWS = range(5, 10)
FIELDS = 10


def at(step, field, lane):
    return (step * FIELDS + field) * PAIR + lane


def table_kernel(slot_count, row_count, group_count, counts, old, new, text, image, out):
    task_count = counts.shape[0]
    half = slot_count // PAIR
    group = lax.axis_index("group")
    first_row = lax.axis_index("seq") * row_count
    size = [counts[t] for t in range(task_count)]
    olds = [old[t] for t in range(task_count)]
    news = [new[t] for t in range(task_count)]
    zero = jnp.int32(0)

    def starts_and_ranks(own):
        starts, ranks = [], []
        for t in range(task_count):
            start, rank = zero, zero
            for u in range(t):
                same = own[u] == own[t]
                start = start + jnp.where(same, size[u], 0)
                rank = rank + jnp.where(same, 1, 0)
            starts.append(start)
            ranks.append(rank)
        return starts, ranks

    old_start, old_rank = starts_and_ranks(olds)
    new_start, new_rank = starts_and_ranks(news)

    def lanes(own, ranks, values):
        found = []
        for lane in range(PAIR):
            value = zero
            for t in range(task_count):
                hit = jnp.logical_and(own[t] == group, ranks[t] == lane)
                value = jnp.where(hit, values[t], value)
            found.append(value)
        return found

    old_size = lanes(olds, old_rank, size)
    old_first = lanes(olds, old_rank, old_start)
    target = lanes(olds, old_rank, news)
    new_size = lanes(news, new_rank, size)
    new_first = lanes(news, new_rank, new_start)
    source = lanes(news, new_rank, olds)
    source_first = lanes(news, new_rank, old_start)
    spare = new_size[0] + new_size[1]
    for step in range(half):
        valid = [step < old_size[lane] for lane in range(PAIR)]
        after = lax.rem(target[1] + 1, group_count)
        first = jnp.where(valid[0], target[0], after)
        second = jnp.where(valid[1], target[1], lax.rem(first + 1, group_count))
        for lane in range(PAIR):
            slot = jnp.where(valid[lane], old_first[lane] + step, 0)
            out[at(step, OLD_VALID, lane)] = jnp.where(valid[lane], 1, 0)
            out[at(step, OLD_SLOT, lane)] = slot
            out[at(step, OLD_TARGET, lane)] = (first, second)[lane]
            out[at(step, OLD_KEYS, lane)] = image[group * slot_count + slot]
            out[at(step, OLD_ROWS, lane)] = text[group * slot_count + slot] - first_row
            here = step < new_size[lane]
            came = source[lane] * slot_count + jnp.where(here, source_first[lane] + step, 0)
            out[at(step, NEW_VALID, lane)] = jnp.where(here, 1, 0)
            out[at(step, NEW_SLOT, lane)] = jnp.where(here, new_first[lane] + step, spare)
            out[at(step, NEW_SOURCE, lane)] = source[lane]
            out[at(step, NEW_KEYS, lane)] = image[came]
            out[at(step, NEW_ROWS, lane)] = text[came] - first_row
            spare = spare + jnp.where(here, 0, 1)


def make_table(slot_count, row_count, group_count, *scalars):
    smem = pl.BlockSpec(memory_space=pltpu.SMEM)
    return pl.pallas_call(
        functools.partial(table_kernel, slot_count, row_count, group_count),
        name="table",
        out_shape=jax.ShapeDtypeStruct((slot_count * FIELDS,), jnp.int32),
        in_specs=[smem] * len(scalars),
        out_specs=smem,
    )(*scalars)


def pack_kernel(table, *refs):
    out_ref = refs[-1]
    first = 0
    for ref in refs[:-1]:
        out_ref[0, first : first + ref.shape[1]] = ref[0]
        first += ref.shape[1]


def pack(table, slot_of, count, *arrays):
    rows = sum(array.shape[1] for array in arrays)
    width = arrays[0].shape[2]
    return pl.pallas_call(
        pack_kernel,
        name="pack",
        out_shape=jax.ShapeDtypeStruct((count, rows, width), arrays[0].dtype),
        grid_spec=pltpu.PrefetchScalarGridSpec(
            num_scalar_prefetch=1,
            grid=(count,),
            in_specs=[
                pl.BlockSpec((1,) + array.shape[1:], lambda i, t: (slot_of(i, t), 0, 0))
                for array in arrays
            ],
            out_specs=pl.BlockSpec((1, rows, width), lambda i, t: (i, 0, 0)),
        ),
        cost_estimate=pl.CostEstimate(
            flops=0, bytes_accessed=4 * count * rows * width, transcendentals=0
        ),
    )(table, *arrays)


def unpack_kernel(table, in_ref, normal_ref, packed_ref):
    rows = normal_ref.shape[1]
    tile = min(rows, 64)
    for first in range(0, rows, tile):
        normal_ref[0, first : first + tile] = normalize(in_ref[0, first : first + tile])
    packed_ref[0] = in_ref[0, rows:]


def unpack(table, step, incoming, rows):
    _, height, width = incoming.shape
    return pl.pallas_call(
        unpack_kernel,
        name="unpack",
        out_shape=(
            jax.ShapeDtypeStruct((PAIR, rows, width), incoming.dtype),
            jax.ShapeDtypeStruct((PAIR, height - rows, width), incoming.dtype),
        ),
        grid_spec=pltpu.PrefetchScalarGridSpec(
            num_scalar_prefetch=1,
            grid=(PAIR,),
            in_specs=[
                pl.BlockSpec(
                    (1, height, width), lambda a, t: (t[at(step, NEW_SOURCE, a)], 0, 0)
                )
            ],
            out_specs=(
                pl.BlockSpec((1, rows, width), lambda a, t: (a, 0, 0)),
                pl.BlockSpec((1, height - rows, width), lambda a, t: (a, 0, 0)),
            ),
        ),
        cost_estimate=pl.CostEstimate(
            flops=8 * PAIR * rows * width,
            bytes_accessed=4 * PAIR * height * width,
            transcendentals=0,
        ),
    )(table, incoming)


def normalize(samples_rows):
    values = samples_rows.astype(jnp.float32)
    average = jnp.mean(values, axis=-1, keepdims=True)
    centred = values - average
    variance = jnp.mean(centred * centred, axis=-1, keepdims=True)
    return (centred * lax.rsqrt(variance + norm_eps)).astype(jnp.bfloat16)


def attend_kernel(fields, table, q_ref, k_ref, v_ref, w_hbm, *rest):
    out_ref, w_ref, ctx_ref, sem = rest[-4:]
    lane = pl.program_id(0)
    rows, width = ctx_ref.shape
    seq_count, piece = k_ref.shape[0], k_ref.shape[1]
    keys = seq_count * piece
    load = pltpu.make_async_copy(w_hbm, w_ref, sem)

    @pl.when(lane == 0)
    def _():
        load.start()

    valid = table[fields[0] + lane] > 0
    key_limit = table[fields[1] + lane]
    row_limit = table[fields[2] + lane]

    @pl.when(valid)
    def _():
        allowed = lax.broadcasted_iota(jnp.int32, (rows, keys), 1) < key_limit

        def some_heads(block, carry):
            for inner in range(HEADS_AT_ONCE):
                first = pl.multiple_of((block * HEADS_AT_ONCE + inner) * HEAD_DIM, HEAD_DIM)
                columns = pl.ds(first, HEAD_DIM)
                key = k_ref[:, :, columns].reshape(keys, HEAD_DIM)
                value = v_ref[:, :, columns].reshape(keys, HEAD_DIM)
                scores = lax.dot_general(
                    q_ref[0, :, columns],
                    key,
                    (((1,), (1,)), ((), ())),
                    preferred_element_type=jnp.float32,
                )
                scores = jnp.where(allowed, scores, masked_score)
                top = jnp.max(scores, axis=-1, keepdims=True)
                probs = jnp.where(allowed, jnp.exp(scores - top), 0.0)
                total = jnp.sum(probs, axis=-1, keepdims=True)
                context = jnp.dot(
                    probs.astype(jnp.bfloat16), value, preferred_element_type=jnp.float32
                )
                ctx_ref[:, columns] = (context / total).astype(jnp.bfloat16)
            return carry

        lax.fori_loop(0, width // (HEAD_DIM * HEADS_AT_ONCE), some_heads, 0)

    @pl.when(lane == 0)
    def _():
        load.wait()

    @pl.when(valid)
    def _():
        features = out_ref.shape[2]
        kept = lax.broadcasted_iota(jnp.int32, (rows, OUT_TILE), 0) < row_limit

        def some_columns(block, carry):
            columns = pl.ds(pl.multiple_of(block * OUT_TILE, OUT_TILE), OUT_TILE)
            projected = jnp.dot(
                ctx_ref[...], w_ref[:, columns], preferred_element_type=jnp.float32
            )
            out_ref[0, :, columns] = jnp.where(kept, projected, 0.0).astype(jnp.bfloat16)
            return carry

        lax.fori_loop(0, features // OUT_TILE, some_columns, 0)

    @pl.when(jnp.logical_not(valid))
    def _():
        out_ref[...] = jnp.zeros_like(out_ref)


def attend(table, step, queries, gathered, w_out, out_count, result=None):
    _, rows, width = queries.shape
    seq_count, packed, _ = gathered.shape
    piece = packed // (2 * PAIR)
    features = w_out.shape[1]
    keys = seq_count * piece
    if result is None:
        names, to = (OLD_VALID, OLD_KEYS, OLD_ROWS), OLD_TARGET
        earlier = ()

        def query_of(a, t):
            return t[at(step, OLD_SLOT, a)], 0, 0
    else:
        names, to = (NEW_VALID, NEW_KEYS, NEW_ROWS), NEW_SLOT
        earlier = (result,)

        def query_of(a, t):
            return a, 0, 0

    fields = tuple(at(step, name, 0) for name in names)
    return pl.pallas_call(
        functools.partial(attend_kernel, fields),
        name="attend",
        out_shape=jax.ShapeDtypeStruct((out_count, rows, features), jnp.bfloat16),
        grid_spec=pltpu.PrefetchScalarGridSpec(
            num_scalar_prefetch=1,
            grid=(PAIR,),
            in_specs=[
                pl.BlockSpec((1, rows, width), query_of),
                pl.BlockSpec((seq_count, piece, width), lambda a, t: (0, 2 * a, 0)),
                pl.BlockSpec((seq_count, piece, width), lambda a, t: (0, 2 * a + 1, 0)),
                pl.BlockSpec(memory_space=pl.ANY),
            ]
            + [pl.BlockSpec(memory_space=pl.ANY)] * len(earlier),
            out_specs=pl.BlockSpec(
                (1, rows, features), lambda a, t: (t[at(step, to, a)], 0, 0)
            ),
            scratch_shapes=[
                pltpu.VMEM(w_out.shape, jnp.bfloat16),
                pltpu.VMEM((rows, width), jnp.bfloat16),
                pltpu.SemaphoreType.DMA,
            ],
        ),
        input_output_aliases={5: 0} if earlier else {},
        compiler_params=pltpu.CompilerParams(
            dimension_semantics=("arbitrary",), vmem_limit_bytes=40 * 1024 * 1024
        ),
        cost_estimate=pl.CostEstimate(
            flops=PAIR * 2 * rows * width * (2 * keys + features),
            bytes_accessed=2 * (w_out.size + PAIR * (2 * rows + 2 * keys) * width),
            transcendentals=PAIR * rows * keys * (width // HEAD_DIM),
        ),
    )(table, queries, gathered, gathered, w_out, *earlier)


def place_kernel(field, table, in_ref, *rest):
    out_ref = rest[-1]
    lane = pl.program_id(0)
    valid = table[field + lane] > 0

    @pl.when(valid)
    def _():
        out_ref[...] = in_ref[...]

    @pl.when(jnp.logical_not(valid))
    def _():
        out_ref[...] = jnp.zeros_like(out_ref)


def place(table, step, incoming, result, slot_count):
    _, rows, features = incoming.shape
    block = (1, rows, features)
    earlier = () if result is None else (result,)
    return pl.pallas_call(
        functools.partial(place_kernel, at(step, NEW_VALID, 0)),
        name="place",
        out_shape=jax.ShapeDtypeStruct((slot_count, rows, features), jnp.bfloat16),
        grid_spec=pltpu.PrefetchScalarGridSpec(
            num_scalar_prefetch=1,
            grid=(PAIR,),
            in_specs=[pl.BlockSpec(block, lambda a, t: (t[at(step, NEW_SOURCE, a)], 0, 0))]
            + [pl.BlockSpec(memory_space=pl.ANY)] * len(earlier),
            out_specs=pl.BlockSpec(block, lambda a, t: (t[at(step, NEW_SLOT, a)], 0, 0)),
        ),
        input_output_aliases={2: 0} if earlier else {},
        compiler_params=pltpu.CompilerParams(dimension_semantics=("arbitrary",)),
        cost_estimate=pl.CostEstimate(
            flops=0, bytes_accessed=4 * PAIR * rows * features, transcendentals=0
        ),
    )(table, incoming, *earlier)


def on_device(
    tokens,
    image_keys,
    image_values,
    text_len,
    image_len,
    counts,
    old_group,
    new_group,
    w_query,
    w_out,
):
    group_count = lax.axis_size("group")
    slot_count, row_count, features = tokens.shape
    half = slot_count // PAIR
    width = w_query.shape[1]
    table = make_table(
        slot_count, row_count, group_count, counts, old_group, new_group, text_len, image_len
    )

    def exchange(blocks):
        return lax.all_to_all(blocks, "group", split_axis=0, concat_axis=0, tiled=True)

    def gather(packed):
        return lax.all_gather(packed.reshape(-1, width), "seq", axis=0, tiled=False)

    def project(normal):
        flat = normal.reshape(-1, features)
        queries = jnp.dot(flat, w_query, preferred_element_type=jnp.float32)
        queries = (queries * HEAD_DIM ** (-0.5)).astype(jnp.bfloat16)
        return queries.reshape(normal.shape[0], row_count, width)

    gathered = {}
    for step in range(1, half):

        def slot_of(lane, t, step=step):
            return t[at(step, OLD_SLOT, lane)]

        gathered[step] = gather(pack(table, slot_of, PAIR, image_keys, image_values))

    def slot_to(group, t):
        to_first = t[at(0, OLD_TARGET, 0)] == group
        return jnp.where(to_first, t[at(0, OLD_SLOT, 0)], t[at(0, OLD_SLOT, 1)])

    moved = exchange(pack(table, slot_to, group_count, tokens, image_keys, image_values))
    queries = project(normalize(tokens))

    result = None
    for step in range(1, half):
        outgoing = attend(table, step, queries, gathered[step], w_out, group_count)
        incoming = exchange(outgoing)
        if step == half - 1:
            normal, packed = unpack(table, 0, moved, row_count)
            result = attend(
                table, 0, project(normal), gather(packed), w_out, slot_count, result
            )
        result = place(table, step, incoming, result, slot_count)
    return result


def solution(mesh):
    rows = P("group", "seq", None)
    return jax.shard_map(
        on_device,
        mesh=mesh,
        in_specs=(rows, rows, rows) + (P(),) * 7,
        out_specs=rows,
        check_vma=False,
    )
```

time: 323 us -> 251 us (0.78)
  waiting for transfers between devices: 147 us -> 78.2 us
  Pallas kernels: 47.2 us -> 80.3 us
  between operations: 28.8 us -> 13.3 us
  other arithmetic: 27.3 us -> 13.1 us
  local copies, waits for them, and re-layouts: 27.5 us -> 14.8 us
  matrix products: 19.5 us -> 30.2 us
  starting transfers between devices: 24.4 us -> 20.4 us
    all_gather x4, waiting for transfers between devices: 65.8 us -> 27.2 us  [gather(): return lax.all_gather(packed.reshape(-1, width), 'seq', axis=0, tiled=False)]
    pallas_call x8 -> x13, Pallas kernels: 47.2 us -> 80.3 us  [the longest x4 52.1 us: attend(): pl.pallas_call(functools.partial(attend_kernel, fields), name='attend', o...]
    all_to_all x4, waiting for transfers between devices: 80.8 us -> 51 us  [exchange(): lax.all_to_all(blocks, 'group', split_axis=0, concat_axis=0, tiled=True)]
    dot_general x1 -> x2, matrix products: 19.5 us -> 30.2 us  [project(): queries = jnp.dot(flat, w_query, preferred_element_type=jnp.float32)]
    squeeze x10 -> x0, local copies, waits for them, and re-layouts: 6.22 us -> none  [the longest x2 3.14 us: on_device(): lax.dynamic_index_in_dim(rows, old_slot[step, lane], 0, keepdims=False)]
    all_to_all x4, starting transfers between devices: 24.3 us -> 20.2 us  [exchange(): lax.all_to_all(blocks, 'group', split_axis=0, concat_axis=0, tiled=True)]
    concatenate x4 -> x0, other arithmetic: 3.53 us -> none  [on_device(): packed = jnp.concatenate(pieces, axis=0)]
    unnamed x26 -> x24, local copies, waits for them, and re-layouts: 16.6 us -> 14.8 us
  transfers between devices with their start and end apart: 8 -> 8, of which waited for: 8 -> 6; matrix products, arithmetic and copies ran while one was open for 14% -> 17% of each run, Pallas kernels for 14% -> 29%
where the time goes in v2:
time: 251 us; the launch traced here: 250 us
  Pallas kernels  80.3 us (32%)
  waiting for transfers between devices  78.2 us (31%)
  matrix products  30.2 us (12%)
  starting transfers between devices  20.4 us (8%)
  local copies, waits for them, and re-layouts  14.8 us (6%)
  between operations  13.3 us (5%)
  other arithmetic  13.1 us (5%)
    pallas_call x4, Pallas kernels, attend(): pl.pallas_call(functools.partial(attend_kernel, fields), name='attend', o...  52.1 us
    all_to_all x4, waiting for transfers between devices, exchange(): lax.all_to_all(blocks, 'group', split_axis=0, concat_axis=0, tiled=True)  51 us
    dot_general x2, matrix products, project(): queries = jnp.dot(flat, w_query, preferred_element_type=jnp.float32)  30.2 us
    all_gather x4, waiting for transfers between devices, gather(): return lax.all_gather(packed.reshape(-1, width), 'seq', axis=0, tiled=False)  27.2 us
    all_to_all x4, starting transfers between devices, exchange(): lax.all_to_all(blocks, 'group', split_axis=0, concat_axis=0, tiled=True)  20.2 us
    unnamed x24, local copies, waits for them, and re-layouts  14.8 us
    pallas_call x4, Pallas kernels, pack(): pl.pallas_call(pack_kernel, name='pack', out_shape=jax.ShapeDtypeStruct((...  12.4 us
    pallas_call x3, Pallas kernels, place(): pl.pallas_call(functools.partial(place_kernel, at(step, NEW_VALID, 0)), n...  10 us
  transfers between devices with their start and end apart: 8, of which 6 were waited for; matrix products, arithmetic and copies ran while one was open for 17% of the time, Pallas kernels for 29%

profile of v2, /device:TPU:0, one launch (start us, length us, event | category | flops | bytes accessed | tf_op | source)
XLA Modules:
  0.0 250.3 jit_solution(3044497048512434756)
XLA Ops:
  8.0 2.5 pack.7
  10.5 2.5 %pack.6 = bf16[2,64,2048]{2,1,0:T(8,128)(2,1)} custom-call(s32[80]{0:T(128)} %table.1, bf16[8,32,2048]{2,1,0:T(8,128)(2,1)} %refs_0_.7, bf16[8,32,2048]{2,1,0:T(8,128)(2,1)} %refs_1_.7), custom_call_target="tpu_custom_call" | custom-call | bytes 1048576 | tf_op jit(solution)/shard_map/pack/pallas_call | solution.py:115
  13.1 4.8 %pack.5 = bf16[4,320,2048]{2,1,0:T(8,128)(2,1)} custom-call(s32[80]{0:T(128)} %table.1, bf16[8,256,2048]{2,1,0:T(8,128)(2,1)} %refs_0_.5, bf16[8,32,2048]{2,1,0:T(8,128)(2,1)} %refs_0_.7, bf16[8,32,2048]{2,1,0:T(8,128)(2,1)} %refs_1_.7), custom_call_target="tpu_custom_call" | custom-call | bytes 10485760 | tf_op jit(solution)/shard_map/pack/pallas_call | solution.py:115
  17.9 5.6 %all-to-all-start.1 = ((bf16[4,320,2048]{2,1,0:T(8,128)(2,1)}), bf16[4,320,2048]{2,1,0:T(8,128)(2,1)}, u32[]{:S(2)}, u32[]{:S(2)}) async-start(bf16[4,320,2048]{2,1,0:T(8,128)(2,1)} %pack.5), calls=%async_computation.1 | async-start | bytes 10485760 | tf_op jit(solution)/shard_map/all_to_all | solution.py:361
  23.4 2.5 %pack.4 = bf16[2,64,2048]{2,1,0:T(8,128)(2,1)} custom-call(s32[80]{0:T(128)} %table.1, bf16[8,32,2048]{2,1,0:T(8,128)(2,1)} %refs_0_.7, bf16[8,32,2048]{2,1,0:T(8,128)(2,1)} %refs_1_.7), custom_call_target="tpu_custom_call" | custom-call | bytes 1048576 | tf_op jit(solution)/shard_map/pack/pallas_call | solution.py:115
  26.0 4.7 %convert_reduce_fusion = f32[8,256]{1,0:T(8,128)S(1)} fusion(bf16[8,256,2048]{2,1,0:T(8,128)(2,1)} %refs_0_.5), kind=kLoop, calls=%fused_computation.1 | loop fusion | flops 8386560 | bytes 8396800 | tf_op jit(solution)/shard_map/reduce_sum | solution.py:174
  30.8 6.0 %fusion.2 = f32[8,256]{1,0:T(8,128)S(1)} fusion(bf16[8,256,2048]{2,1,0:T(8,128)(2,1)} %refs_0_.5, f32[8,256]{1,0:T(8,128)S(1)} %broadcast_multiply_fusion), kind=kLoop, calls=%fused_computation.4 | loop fusion | flops 16775168 | bytes 8404992 | tf_op jit(solution)/shard_map/reduce_sum | solution.py:176
  36.8 2.4 fusion.3
  39.2 21.6 %multiply_convert_fusion = bf16[2048,2048]{1,0:T(8,128)(2,1)} fusion(bf16[2048,2048]{1,0:T(8,128)(2,1)S(1)} %bitcast.18, bf16[2048,2048]{1,0:T(8,128)(2,1)} %param.18), kind=kOutput, calls=%fused_computation.6 | convolution fusion | flops 17188257792 | bytes 25165824 | tf_op jit(solution)/shard_map/dot_general | solution.py:368
  60.8 2.2 copy-done.6
  63.0 14.6 %attend.6 = bf16[4,256,2048]{2,1,0:T(8,128)(2,1)S(1)} custom-call(s32[80]{0:T(128)S(1)} %copy-done.7, bf16[8,256,2048]{2,1,0:T(8,128)(2,1)} %bitcast.15, bf16[8,128,2048]{2,1,0:T(8,128)(2,1)S(1)} %copy-done.6, bf16[8,128,2048]{2,1,0:T(8,128)(2,1)S(1)} %copy-done.6, bf16[2048,2048]{1,0:T(8,128)(2,1)} %w_hbm.7), custom_call_target="tpu_custom_call" | custom-call | flops 5368709120 | bytes 16777216 | tf_op jit(solution)/shard_map/attend/pallas_call | solution.py:268
  79.6 4.4 %all-to-all-done.1.in_ref = bf16[4,320,2048]{2,1,0:T(8,128)(2,1)} async-done(((bf16[4,320,2048]{2,1,0:T(8,128)(2,1)}), bf16[4,320,2048]{2,1,0:T(8,128)(2,1)}, u32[]{:S(2)}, u32[]{:S(2)}) %all-to-all-start.1) | async-done | bytes 5242912 | tf_op jit(solution)/shard_map/all_to_all | solution.py:361
  84.1 4.9 %all-to-all-start.3 = ((bf16[4,256,2048]{2,1,0:T(8,128)(2,1)}), bf16[4,256,2048]{2,1,0:T(8,128)(2,1)}, u32[]{:S(2)}, u32[]{:S(2)}) async-start(bf16[4,256,2048]{2,1,0:T(8,128)(2,1)} %copy-done.1), calls=%async_computation.3 | async-start | bytes 8388608 | tf_op jit(solution)/shard_map/all_to_all | solution.py:361
  89.2 4.3 %unpack.1 = (bf16[2,256,2048]{2,1,0:T(8,128)(2,1)}, bf16[2,64,2048]{2,1,0:T(8,128)(2,1)}) custom-call(s32[80]{0:T(128)} %table.1, bf16[4,320,2048]{2,1,0:T(8,128)(2,1)} %all-to-all-done.1.in_ref), custom_call_target="tpu_custom_call" | custom-call | flops 8388608 | bytes 5242880 | tf_op jit(solution)/shard_map/unpack/pallas_call | solution.py:144
  93.5 14.0 %all-gather.9.cloned.1.call-done.k_ref.v_ref = bf16[8,128,2048]{2,1,0:T(8,128)(2,1)} async-done(((bf16[1,128,2048]{2,1,0:T(8,128)(2,1)}), bf16[8,128,2048]{2,1,0:T(8,128)(2,1)}) %all-gather.9.cloned.1.call-update) | async-done | bytes 4194320 | tf_op jit(solution)/shard_map/all_gather | solution.py:364
  107.5 2.2 copy-done.4
  109.7 14.5 %attend.5 = bf16[4,256,2048]{2,1,0:T(8,128)(2,1)S(1)} custom-call(s32[80]{0:T(128)S(1)} %copy-done.8, bf16[8,256,2048]{2,1,0:T(8,128)(2,1)} %bitcast.16, bf16[8,128,2048]{2,1,0:T(8,128)(2,1)S(1)} %copy-done.4, bf16[8,128,2048]{2,1,0:T(8,128)(2,1)S(1)} %copy-done.4, bf16[2048,2048]{1,0:T(8,128)(2,1)} %w_hbm.7), custom_call_target="tpu_custom_call" | custom-call | flops 5368709120 | bytes 16777216 | tf_op jit(solution)/shard_map/attend/pallas_call | solution.py:268
  124.3 2.0 copy-done.3
  126.3 10.5 %all-to-all-done.3.in_ref = bf16[4,256,2048]{2,1,0:T(8,128)(2,1)} async-done(((bf16[4,256,2048]{2,1,0:T(8,128)(2,1)}), bf16[4,256,2048]{2,1,0:T(8,128)(2,1)}, u32[]{:S(2)}, u32[]{:S(2)}) %all-to-all-start.3) | async-done | bytes 4194336 | tf_op jit(solution)/shard_map/all_to_all | solution.py:361
  136.8 4.9 %all-to-all-start.2 = ((bf16[4,256,2048]{2,1,0:T(8,128)(2,1)}), bf16[4,256,2048]{2,1,0:T(8,128)(2,1)}, u32[]{:S(2)}, u32[]{:S(2)}) async-start(bf16[4,256,2048]{2,1,0:T(8,128)(2,1)} %copy-done.3), calls=%async_computation.2 | async-start | bytes 8388608 | tf_op jit(solution)/shard_map/all_to_all | solution.py:361
  141.7 13.2 %all-gather.5.cloned.1.call-done.k_ref.v_ref = bf16[8,128,2048]{2,1,0:T(8,128)(2,1)} async-done(((bf16[1,128,2048]{2,1,0:T(8,128)(2,1)}), bf16[8,128,2048]{2,1,0:T(8,128)(2,1)}) %all-gather.5.cloned.1.call-update) | async-done | bytes 4194320 | tf_op jit(solution)/shard_map/all_gather | solution.py:364
  154.9 2.2 copy-done.5
  157.0 14.5 %attend.4 = bf16[4,256,2048]{2,1,0:T(8,128)(2,1)S(1)} custom-call(s32[80]{0:T(128)S(1)} %copy-done.8, bf16[8,256,2048]{2,1,0:T(8,128)(2,1)} %bitcast.17, bf16[8,128,2048]{2,1,0:T(8,128)(2,1)S(1)} %copy-done.5, bf16[8,128,2048]{2,1,0:T(8,128)(2,1)S(1)} %copy-done.5, bf16[2048,2048]{1,0:T(8,128)(2,1)} %w_hbm.7), custom_call_target="tpu_custom_call" | custom-call | flops 5368709120 | bytes 16777216 | tf_op jit(solution)/shard_map/attend/pallas_call | solution.py:268
  173.6 15.1 %all-to-all-done.2.in_ref = bf16[4,256,2048]{2,1,0:T(8,128)(2,1)} async-done(((bf16[4,256,2048]{2,1,0:T(8,128)(2,1)}), bf16[4,256,2048]{2,1,0:T(8,128)(2,1)}, u32[]{:S(2)}, u32[]{:S(2)}) %all-to-all-start.2) | async-done | bytes 4194336 | tf_op jit(solution)/shard_map/all_to_all | solution.py:361
  188.7 4.9 %all-to-all-start = ((bf16[4,256,2048]{2,1,0:T(8,128)(2,1)}), bf16[4,256,2048]{2,1,0:T(8,128)(2,1)}, u32[]{:S(2)}, u32[]{:S(2)}) async-start(bf16[4,256,2048]{2,1,0:T(8,128)(2,1)} %copy-done.2), calls=%async_computation | async-start | bytes 8388608 | tf_op jit(solution)/shard_map/all_to_all | solution.py:361
  193.6 8.6 %multiply_convert_fusion.1 = bf16[512,2048]{1,0:T(8,128)(2,1)S(1)} fusion(bf16[512,2048]{1,0:T(8,128)(2,1)} %bitcast.23, bf16[2048,2048]{1,0:T(8,128)(2,1)} %param.18), kind=kOutput, calls=%fused_computation.7 | convolution fusion | flops 4297064448 | bytes 12582912 | tf_op jit(solution)/shard_map/dot_general | solution.py:368
  202.2 3.3 %place.3.rest_0_ = bf16[8,256,2048]{2,1,0:T(8,128)(2,1)} custom-call(s32[80]{0:T(128)} %table.1, bf16[4,256,2048]{2,1,0:T(8,128)(2,1)} %all-to-all-done.3.in_ref), custom_call_target="tpu_custom_call" | custom-call | bytes 4194304 | tf_op jit(solution)/shard_map/place/pallas_call | solution.py:321
  205.5 3.4 %place.4.rest_0_ = bf16[8,256,2048]{2,1,0:T(8,128)(2,1)} custom-call(s32[80]{0:T(128)} %table.1, bf16[4,256,2048]{2,1,0:T(8,128)(2,1)} %all-to-all-done.2.in_ref, bf16[8,256,2048]{2,1,0:T(8,128)(2,1)} %place.3.rest_0_), custom_call_target="tpu_custom_call", output_to_operand_aliasing={{}: (2, {})} | custom-call | bytes 4194304 | tf_op jit(solution)/shard_map/place/pallas_call | solution.py:321
  208.9 2.2 copy-done
  211.1 8.5 %attend.7.rest_0_ = bf16[8,256,2048]{2,1,0:T(8,128)(2,1)} custom-call(s32[80]{0:T(128)S(1)} %copy-done.9, bf16[2,256,2048]{2,1,0:T(8,128)(2,1)S(1)} %bitcast.12, bf16[8,128,2048]{2,1,0:T(8,128)(2,1)S(1)} %copy-done, bf16[8,128,2048]{2,1,0:T(8,128)(2,1)S(1)} %copy-done, bf16[2048,2048]{1,0:T(8,128)(2,1)} %w_hbm.7, ...), custom_call_target="tpu_custom_call", output_to_operand_aliasing={{}: (5, {})} | custom-call | flops 5368709120 | bytes 16777216 | tf_op jit(solution)/shard_map/attend/pallas_call | solution.py:268
  219.6 20.9 %all-to-all-done.in_ref = bf16[4,256,2048]{2,1,0:T(8,128)(2,1)} async-done(((bf16[4,256,2048]{2,1,0:T(8,128)(2,1)}), bf16[4,256,2048]{2,1,0:T(8,128)(2,1)}, u32[]{:S(2)}, u32[]{:S(2)}) %all-to-all-start) | async-done | bytes 4194336 | tf_op jit(solution)/shard_map/all_to_all | solution.py:361
  240.5 3.3 %place.5 = bf16[8,256,2048]{2,1,0:T(8,128)(2,1)} custom-call(s32[80]{0:T(128)} %table.1, bf16[4,256,2048]{2,1,0:T(8,128)(2,1)} %all-to-all-done.in_ref, bf16[8,256,2048]{2,1,0:T(8,128)(2,1)} %attend.7.rest_0_), custom_call_target="tpu_custom_call", output_to_operand_aliasing={{}: (2, {})} | custom-call | bytes 4194304 | tf_op jit(solution)/shard_map/place/pallas_call | solution.py:321
  (33 shorter events, 5.8 us)
Async XLA Ops:
  6.5 54.3 %all-gather.11.cloned.1.call-start = ((), (), s32[]{:S(2)}) async-start(), calls=%async_computation.7 | async-start | bytes 4718592 | tf_op jit(solution)/shard_map/all_gather | solution.py:364
  10.5 97.0 %all-gather.9.cloned.1.call-start = ((), (), s32[]{:S(2)}) async-start(), calls=%async_computation.6 | async-start | bytes 4718592 | tf_op jit(solution)/shard_map/all_gather | solution.py:364
  17.9 66.2 %all-to-all-start.1 = ((bf16[4,320,2048]{2,1,0:T(8,128)(2,1)}), bf16[4,320,2048]{2,1,0:T(8,128)(2,1)}, u32[]{:S(2)}, u32[]{:S(2)}) async-start(bf16[4,320,2048]{2,1,0:T(8,128)(2,1)} %pack.5), calls=%async_computation.1 | async-start | bytes 10485760 | tf_op jit(solution)/shard_map/all_to_all | solution.py:361
  23.4 131.4 %all-gather.5.cloned.1.call-start = ((), (), s32[]{:S(2)}) async-start(), calls=%async_computation.4 | async-start | bytes 4718592 | tf_op jit(solution)/shard_map/all_gather | solution.py:364
  26.0 10.8 %slice-start = ((s8[8388608]{0:T(1024)(128)(4,1)}), s8[4194304]{0:T(1024)(128)(4,1)S(1)}, s32[]{:S(2)}) async-start(s8[8388608]{0:T(1024)(128)(4,1)} %bitcast.13), calls=%async_computation.8 | async-start | bytes 8388608
  30.8 6.0 %slice-start.1 = ((s8[8388608]{0:T(1024)(128)(4,1)}), s8[4194304]{0:T(1024)(128)(4,1)S(1)}, s32[]{:S(2)}) async-start(s8[8388608]{0:T(1024)(128)(4,1)} %bitcast.13), calls=%async_computation.9 | async-start | bytes 8388608
  39.2 21.6 %copy-start.7 = (s32[80]{0:T(128)S(1)}, s32[80]{0:T(128)}, u32[]{:S(2)}) copy-start(s32[80]{0:T(128)} %table.1) | copy-start | bytes 964
  60.8 2.2 copy-start.6
  77.6 2.0 copy-start.1
  79.6 27.9 %copy-start.8 = (s32[80]{0:T(128)S(1)}, s32[80]{0:T(128)}, u32[]{:S(2)}) copy-start(s32[80]{0:T(128)} %table.1) | copy-start | bytes 964
  84.1 52.7 %all-to-all-start.3 = ((bf16[4,256,2048]{2,1,0:T(8,128)(2,1)}), bf16[4,256,2048]{2,1,0:T(8,128)(2,1)}, u32[]{:S(2)}, u32[]{:S(2)}) async-start(bf16[4,256,2048]{2,1,0:T(8,128)(2,1)} %copy-done.1), calls=%async_computation.3 | async-start | bytes 8388608 | tf_op jit(solution)/shard_map/all_to_all | solution.py:361
  88.9 120.0 %all-gather.7.cloned.1.call-start = ((), (), s32[]{:S(2)}) async-start(), calls=%async_computation.5 | async-start | bytes 4718592 | tf_op jit(solution)/shard_map/all_gather | solution.py:364
  107.5 2.2 copy-start.4
  124.3 2.1 copy-start.3
  136.8 51.9 %all-to-all-start.2 = ((bf16[4,256,2048]{2,1,0:T(8,128)(2,1)}), bf16[4,256,2048]{2,1,0:T(8,128)(2,1)}, u32[]{:S(2)}, u32[]{:S(2)}) async-start(bf16[4,256,2048]{2,1,0:T(8,128)(2,1)} %copy-done.3), calls=%async_computation.2 | async-start | bytes 8388608 | tf_op jit(solution)/shard_map/all_to_all | solution.py:361
  154.9 2.2 copy-start.5
  171.6 2.0 copy-start.2
  188.7 51.8 %all-to-all-start = ((bf16[4,256,2048]{2,1,0:T(8,128)(2,1)}), bf16[4,256,2048]{2,1,0:T(8,128)(2,1)}, u32[]{:S(2)}, u32[]{:S(2)}) async-start(bf16[4,256,2048]{2,1,0:T(8,128)(2,1)} %copy-done.2), calls=%async_computation | async-start | bytes 8388608 | tf_op jit(solution)/shard_map/all_to_all | solution.py:361
  205.5 3.4 %copy-start.9 = (s32[80]{0:T(128)S(1)}, s32[80]{0:T(128)}, u32[]{:S(2)}) copy-start(s32[80]{0:T(128)} %table.1) | copy-start | bytes 964
  208.9 2.2 copy-start
Sparse Core Ops, SparseCore 0:
  10.6 49.5 all-gather.10
  61.8 45.6 all-gather.8
  109.1 45.6 all-gather.4
  156.3 45.7 all-gather.6
